TPU v7x, 32 devices: a whole 2x2x4 slice. The times are simulated.
32 devices in a mesh: grp: 8 (over z, x), lane: 4 (over y, core).
Axes of the slice: x: 2, y: 2, z: 4, core: 2. Of those that a mesh axis runs over, the one named last changes fastest.
Arguments:
- features: bfloat16 [65536, 128], P(('grp', 'lane')), may hold values from -600 to 600
- tiles: bfloat16 [512, 7, 128, 128], P(('grp', 'lane')), may hold values from -0.125 to 0.125
- tile_cols: int32 [512, 7], P(('grp', 'lane')), may hold values from 0 to 23
- send_index: int32 [32, 2, 512], P(('grp', 'lane')), may hold values from 0 to 2047
- send_count: int32 [32, 2], P(('grp', 'lane')), may hold values from 128 to 512, as said below
- coef: float32 [4, 128], replicated, may hold values from -1 to 1
- dest_lane: int32 [65536], P(('grp', 'lane')), may hold values from 0 to 3, as said below
- dest_slot: int32 [65536], P(('grp', 'lane')), may hold values from 0 to 2047, as said below
Outputs:
- table_out: bfloat16 [65536, 128], P(('grp', 'lane'))
Inputs may be any that keep to these rules, and one draw needn't show every extreme that they name: `send_count`: in every draw for each of the two directions some partition has exactly 512 live rows towards that neighbour. `dest_lane`: within each relayout group every row of every table shard is named by exactly one node; at most 1024 rows of one partition go to one shard, and exactly 1024 for some pair in every group. `dest_slot`: together with dest_lane, a one-to-one map of a group's nodes onto its table rows.
All inputs are finite; a program needn't handle non-finite values.
Results may differ from a plain program's by a relative error of at most 0.008.
Values may be sent and summed in bfloat16 or wider, within the bound.
A program may use at most 64 MiB of HBM per device.

v0:
```python
import jax
import jax.numpy as jnp
from jax import lax
from jax.sharding import PartitionSpec as P

ORDER = 3


def from_behind(value, axis, by):
    devices = lax.axis_size(axis)
    return lax.ppermute(value, axis, [(i, (i + by) % devices) for i in range(devices)])


def to_ball(white, feature_width):
    norms = jnp.sqrt(jnp.sum(white * white, axis=1, keepdims=True) + 1e-06)
    radius = jnp.sqrt(jnp.float32(feature_width))
    return (jnp.tanh(norms / radius) * radius * white / norms).astype(jnp.bfloat16)


def whiten(values, factor, node_total):
    solved = jax.scipy.linalg.solve_triangular(factor, values.T, lower=True).T
    return solved * jnp.sqrt(jnp.float32(node_total))


def pack_rows(values, destination, slot_ids, lanes, capacity):
    row_count = values.shape[0]
    onehot = (destination[:, None] == jnp.arange(lanes)[None, :]).astype(jnp.int32)
    rank_in_run = jnp.sum(jnp.cumsum(onehot, axis=0) * onehot, axis=1) - 1
    position = destination * capacity + rank_in_run
    buffer = jnp.zeros((lanes * capacity, values.shape[1]), values.dtype).at[position].set(values)
    slot_buffer = jnp.full((lanes * capacity,), row_count, jnp.int32).at[position].set(slot_ids)
    return (buffer.reshape(lanes, capacity, values.shape[1]), slot_buffer.reshape(lanes, capacity))


def place_rows(received, received_slots, row_count):
    flat_slots = received_slots.reshape(-1)
    empty = jnp.zeros((row_count, received.shape[-1]), jnp.bfloat16)
    return empty.at[flat_slots].set(received, mode="drop")


def body(features, tiles, tile_cols, send_index, send_count, coef, dest_lane, dest_slot):
    row_count, feature_width = features.shape
    tile_size = tiles.shape[2]
    lanes = lax.axis_size("lane")
    node_total = row_count * lax.axis_size("grp") * lanes
    capacity = 2 * row_count // lanes
    boundary = send_index.shape[2]
    valid_rows = jnp.arange(boundary)[None, :] < send_count[0][:, None]

    def operate(current):
        upward = jnp.where(
            valid_rows[0][:, None], current[send_index[0, 0]], jnp.zeros((), jnp.bfloat16)
        )
        downward = jnp.where(
            valid_rows[1][:, None], current[send_index[0, 1]], jnp.zeros((), jnp.bfloat16)
        )
        from_lower = from_behind(upward, "grp", 1)
        from_upper = from_behind(downward, "grp", -1)
        extended = jnp.concatenate([current, from_lower, from_upper], axis=0).reshape(
            -1, tile_size, feature_width
        )
        blocks = extended[tile_cols]
        product = jnp.einsum("bkij,bkjf->bif", tiles, blocks, preferred_element_type=jnp.float32)
        return product.reshape(row_count, feature_width)

    def next_term(cheb_terms):
        if len(cheb_terms) == 1:
            return operate(cheb_terms[0]).astype(jnp.bfloat16)
        return (2.0 * operate(cheb_terms[-1]) - cheb_terms[-2].astype(jnp.float32)).astype(
            jnp.bfloat16
        )

    cheb_terms = [features]
    for term_order in range(1, ORDER):
        cheb_terms.append(next_term(cheb_terms))
    cheb_terms.append(next_term(cheb_terms))
    mixed = jnp.zeros((row_count, feature_width), jnp.float32)
    for term_order in range(ORDER + 1):
        mixed = mixed + coef[term_order][None, :] * cheb_terms[term_order].astype(jnp.float32)
    raw_buffer, raw_slots = pack_rows(mixed, dest_lane, dest_slot, lanes, capacity)
    received_raw, received_slots = (
        lax.all_to_all(raw_buffer, "lane", split_axis=0, concat_axis=0, tiled=True),
        lax.all_to_all(raw_slots, "lane", split_axis=0, concat_axis=0, tiled=True),
    )
    local_gram = jnp.einsum("rf,rg->fg", mixed, mixed, precision=lax.Precision.HIGHEST)
    gram = lax.psum(local_gram, ("grp", "lane"))
    factor = jnp.linalg.cholesky(gram)
    flat_raw = received_raw.reshape(-1, feature_width)
    ball_rows = to_ball(whiten(flat_raw, factor, node_total), feature_width)
    return place_rows(ball_rows, received_slots, row_count)


def solution(mesh):
    placed = (
        P(("grp", "lane"), None),
        P(("grp", "lane"), None, None, None),
        P(("grp", "lane"), None),
        P(("grp", "lane"), None, None),
        P(("grp", "lane"), None),
        P(),
        P(("grp", "lane")),
        P(("grp", "lane")),
    )
    return jax.shard_map(
        body, mesh=mesh, in_specs=placed, out_specs=P(("grp", "lane"), None), check_vma=False
    )
```

profile of v0, /device:TPU:1, one launch (start us, length us, event | category | flops | bytes accessed | tf_op | source)
XLA Modules:
  0.0 245.4 jit_solution(8330663186755694221)
XLA Ops:
  6.5 0.8 compare_select_fusion.3
  8.1 2.2 gather_fusion
  10.4 2.1 collective-permute-start
  12.5 1.3 gather_fusion.1
  14.0 3.1 %collective-permute-start.1 = (bf16[512,128]{1,0:T(8,128)(2,1)S(1)}, bf16[512,128]{1,0:T(8,128)(2,1)S(1)}, u32[]{:S(2)}, u32[]{:S(2)}) collective-permute-start(bf16[512,128]{1,0:T(8,128)(2,1)S(1)} %broadcast_select_fusion.2), channel_id=1, source_target_pairs={{0,28},{4,0},{8,4},{12,8},{16,12},{20,16},{24,20},{28,24},{1,29},{... | collective-permute-start | bytes 393224 | tf_op jit(solution)/shard_map/ppermute | solution.py:11
  17.3 1.2 reduce-window.6
  19.0 3.2 %collective-permute-done.1 = bf16[512,128]{1,0:T(8,128)(2,1)S(1)} collective-permute-done((bf16[512,128]{1,0:T(8,128)(2,1)S(1)}, bf16[512,128]{1,0:T(8,128)(2,1)S(1)}, u32[]{:S(2)}, u32[]{:S(2)}) %collective-permute-start.1) | collective-permute-done | bytes 131104 | tf_op jit(solution)/shard_map/ppermute | solution.py:11
  22.3 2.9 %gather_fusion.2 = bf16[112,128,128]{2,1,0:T(8,128)(2,1)} fusion(bf16[24,128,128]{2,1,0:T(8,128)(2,1)S(1)} %bitcast.98, s32[1024]{0:T(1024)S(1)} %pad_clamp_fusion), kind=kCustom, calls=%fused_computation.2 | custom fusion | bytes 7340480 | tf_op jit(solution)/shard_map/gather | solution.py:62
  25.2 4.3 %fusion.2 = bf16[16,128,128]{1,2,0:T(8,128)(2,1)S(1)} fusion(bf16[16,7,128,128]{3,2,1,0:T(8,128)(2,1)} %param.9, bf16[16,7,128,128]{3,2,1,0:T(8,128)(2,1)} %bitcast.94), kind=kOutput, calls=%fused_computation.23 | convolution fusion | flops 470024192 | bytes 7864320 | tf_op jit(solution)/shard_map/bkij,bkjf->bif/dot_general | solution.py:63
  29.4 1.3 gather_fusion.3
  30.8 1.3 gather_fusion.4
  32.5 4.2 %collective-permute-start.3 = (bf16[512,128]{1,0:T(8,128)(2,1)S(1)}, bf16[512,128]{1,0:T(8,128)(2,1)S(1)}, u32[]{:S(2)}, u32[]{:S(2)}) collective-permute-start(bf16[512,128]{1,0:T(8,128)(2,1)S(1)} %broadcast_select_fusion.1), channel_id=1, source_target_pairs={{0,28},{4,0},{8,4},{12,8},{16,12},{20,16},{24,20},{28,24},{1,29},{... | collective-permute-start | bytes 393224 | tf_op jit(solution)/shard_map/ppermute | solution.py:11
  36.7 8.8 %scatter_custom_fusion = s32[4096]{0:T(1024)} fusion(s32[2048]{0:T(1024)S(1)} %compare_select_fusion.1, s32[2048]{0:T(1024)} %param.15, s32[]{:T(128)} %constant.66.clone.1), kind=kCustom, calls=%fused_computation.66 | custom fusion | bytes 16896 | tf_op jit(solution)/shard_map/scatter | solution.py:31
  45.5 4.3 %all-to-all-start = ((s32[4,1,1024]{2,1,0:T(1,128)}), s32[4,1,1024]{2,1,0:T(1,128)S(1)}, u32[]{:S(2)}, u32[]{:S(2)}) async-start(s32[4,1,1024]{2,1,0:T(1,128)} %bitcast.2), calls=%async_computation | async-start | bytes 32768 | tf_op jit(solution)/shard_map/all_to_all | solution.py:83
  49.8 2.9 %gather_fusion.5 = bf16[112,128,128]{2,1,0:T(8,128)(2,1)} fusion(bf16[24,128,128]{2,1,0:T(8,128)(2,1)S(1)} %bitcast.99, s32[1024]{0:T(1024)S(1)} %pad_clamp_fusion), kind=kCustom, calls=%fused_computation.5 | custom fusion | bytes 7340480 | tf_op jit(solution)/shard_map/gather | solution.py:62
  52.7 4.3 %fusion = f32[16,128,128]{1,2,0:T(8,128)S(1)} fusion(bf16[16,7,128,128]{3,2,1,0:T(8,128)(2,1)} %param.9, bf16[16,7,128,128]{3,2,1,0:T(8,128)(2,1)} %bitcast.96), kind=kOutput, calls=%fused_computation.17 | convolution fusion | flops 470024192 | bytes 8388608 | tf_op jit(solution)/shard_map/bkij,bkjf->bif/dot_general | solution.py:63
  57.1 1.3 gather_fusion.6
  58.5 1.3 gather_fusion.7
  60.2 4.4 %collective-permute-start.5 = (bf16[512,128]{1,0:T(8,128)(2,1)S(1)}, bf16[512,128]{1,0:T(8,128)(2,1)S(1)}, u32[]{:S(2)}, u32[]{:S(2)}) collective-permute-start(bf16[512,128]{1,0:T(8,128)(2,1)S(1)} %broadcast_select_fusion), channel_id=1, source_target_pairs={{0,28},{4,0},{8,4},{12,8},{16,12},{20,16},{24,20},{28,24},{1,29},{... | collective-permute-start | bytes 393224 | tf_op jit(solution)/shard_map/ppermute | solution.py:11
  64.6 3.2 %collective-permute-done.4 = bf16[512,128]{1,0:T(8,128)(2,1)S(1)} collective-permute-done((bf16[512,128]{1,0:T(8,128)(2,1)S(1)}, bf16[512,128]{1,0:T(8,128)(2,1)S(1)}, u32[]{:S(2)}, u32[]{:S(2)}) %collective-permute-start.4) | collective-permute-done | bytes 131104 | tf_op jit(solution)/shard_map/ppermute | solution.py:11
  67.8 2.9 %gather_fusion.8 = bf16[112,128,128]{2,1,0:T(8,128)(2,1)} fusion(bf16[24,128,128]{2,1,0:T(8,128)(2,1)S(1)} %bitcast.97, s32[1024]{0:T(1024)S(1)} %pad_clamp_fusion), kind=kCustom, calls=%fused_computation.8 | custom fusion | bytes 7340480 | tf_op jit(solution)/shard_map/gather | solution.py:62
  70.7 4.3 %fusion.1 = f32[16,128,128]{1,2,0:T(8,128)S(1)} fusion(bf16[16,7,128,128]{3,2,1,0:T(8,128)(2,1)} %param.9, bf16[16,7,128,128]{3,2,1,0:T(8,128)(2,1)} %bitcast.95), kind=kOutput, calls=%fused_computation.18 | convolution fusion | flops 470024192 | bytes 8388608 | tf_op jit(solution)/shard_map/bkij,bkjf->bif/dot_general | solution.py:63
  75.4 2.4 fusion.21
  77.9 7.0 %scatter_custom_fusion.1 = f32[4096,128]{1,0:T(8,128)} fusion(s32[2048]{0:T(1024)S(1)} %compare_select_fusion.1, f32[2048,128]{1,0:T(8,128)S(1)} %fusion.5, f32[]{:T(128)} %constant.71.clone.1), kind=kCustom, calls=%fused_computation.29 | custom fusion | bytes 2097156 | tf_op jit(solution)/shard_map/scatter | solution.py:30
  84.9 4.9 %all-to-all-start.1 = ((f32[4,1024,128]{2,1,0:T(8,128)}), f32[4,1024,128]{2,1,0:T(8,128)S(1)}, u32[]{:S(2)}, u32[]{:S(2)}) async-start(f32[4,1024,128]{2,1,0:T(8,128)} %bitcast.100), calls=%async_computation.1 | async-start | bytes 4194304 | tf_op jit(solution)/shard_map/all_to_all | solution.py:82
  89.9 109.3 %all-reduce.2.cloned.1.call-done = f32[128,128]{0,1:T(8,128)} async-done(((f32[128,128]{0,1:T(8,128)}), f32[128,128]{0,1:T(8,128)}) %all-reduce.2.cloned.1.call-update) | async-done | bytes 65552 | tf_op jit(solution)/shard_map/psum | solution.py:86
  199.2 0.9 copy.14
  200.1 0.9 fusion.15
  201.0 11.7 %cholesky.16 = f32[128,128]{1,0:T(8,128)S(1)} custom-call(f32[128,128]{1,0:T(8,128)S(1)} %fusion.15), custom_call_target="Cholesky" | custom-call | tf_op jit(solution)/shard_map/jit(cholesky)/cholesky | solution.py:87
  214.1 9.8 %custom-call.7 = f32[1,128,128]{1,2,0:T(8,128)S(1)} custom-call(f32[1,128,128]{2,1,0:T(8,128)S(1)} %fusion.12), custom_call_target="InvertDiagBlocksLowerTriangular" | custom-call | tf_op jit(solution)/shard_map/jit(_solve_triangular)/triangular_solve | solution.py:21
  223.9 2.2 multiply_reduce_fusion
  227.0 11.6 %scatter_custom_fusion.2 = bf16[2048,128]{1,0:T(8,128)(2,1)} fusion(s32[4096]{0:T(1024)S(1)} %bitcast.104, bf16[4096,128]{1,0:T(8,128)(2,1)S(1)} %copy.15, bf16[]{:T(256)} %constant.65.clone.1), kind=kCustom, calls=%fused_computation.34 | custom fusion | bytes 524290 | tf_op jit(solution)/shard_map/scatter | solution.py:38
  (51 shorter events, 5.5 us)
Async XLA Ops:
  6.5 6.0 %copy-start = (bf16[2048,128]{1,0:T(8,128)(2,1)S(1)}, bf16[2048,128]{1,0:T(8,128)(2,1)}, u32[]{:S(2)}) copy-start(bf16[2048,128]{1,0:T(8,128)(2,1)} %param.8) | copy-start | bytes 1572868
  6.5 10.6 %copy-start.2 = (s32[16,7]{0,1:T(8,128)S(1)}, s32[16,7]{0,1:T(8,128)}, u32[]{:S(2)}) copy-start(s32[16,7]{0,1:T(8,128)} %param.10) | copy-start | bytes 1348
  6.5 10.8 %copy-start.1 = (s32[2048]{0:T(1024)S(1)}, s32[2048]{0:T(1024)}, u32[]{:S(2)}) copy-start(s32[2048]{0:T(1024)} %param.14) | copy-start | bytes 24580
  10.4 8.6 %collective-permute-start = (bf16[512,128]{1,0:T(8,128)(2,1)S(1)}, bf16[512,128]{1,0:T(8,128)(2,1)S(1)}, u32[]{:S(2)}, u32[]{:S(2)}) collective-permute-start(bf16[512,128]{1,0:T(8,128)(2,1)S(1)} %broadcast_select_fusion.5), channel_id=1, source_target_pairs={{0,4},{4,8},{8,12},{12,16},{16,20},{20,24},{24,28},{28,0},{1,5},{5... | collective-permute-start | bytes 393224 | tf_op jit(solution)/shard_map/ppermute | solution.py:11
  14.0 8.3 %collective-permute-start.1 = (bf16[512,128]{1,0:T(8,128)(2,1)S(1)}, bf16[512,128]{1,0:T(8,128)(2,1)S(1)}, u32[]{:S(2)}, u32[]{:S(2)}) collective-permute-start(bf16[512,128]{1,0:T(8,128)(2,1)S(1)} %broadcast_select_fusion.2), channel_id=1, source_target_pairs={{0,28},{4,0},{8,4},{12,8},{16,12},{20,16},{24,20},{28,24},{1,29},{... | collective-permute-start | bytes 393224 | tf_op jit(solution)/shard_map/ppermute | solution.py:11
  32.3 17.5 %collective-permute-start.2 = (bf16[512,128]{1,0:T(8,128)(2,1)S(1)}, bf16[512,128]{1,0:T(8,128)(2,1)S(1)}, u32[]{:S(2)}, u32[]{:S(2)}) collective-permute-start(bf16[512,128]{1,0:T(8,128)(2,1)S(1)} %broadcast_select_fusion.4), channel_id=1, source_target_pairs={{0,4},{4,8},{8,12},{12,16},{16,20},{20,24},{24,28},{28,0},{1,5},{5... | collective-permute-start | bytes 393224 | tf_op jit(solution)/shard_map/ppermute | solution.py:11
  32.5 17.3 %collective-permute-start.3 = (bf16[512,128]{1,0:T(8,128)(2,1)S(1)}, bf16[512,128]{1,0:T(8,128)(2,1)S(1)}, u32[]{:S(2)}, u32[]{:S(2)}) collective-permute-start(bf16[512,128]{1,0:T(8,128)(2,1)S(1)} %broadcast_select_fusion.1), channel_id=1, source_target_pairs={{0,28},{4,0},{8,4},{12,8},{16,12},{20,16},{24,20},{28,24},{1,29},{... | collective-permute-start | bytes 393224 | tf_op jit(solution)/shard_map/ppermute | solution.py:11
  45.5 39.4 %all-to-all-start = ((s32[4,1,1024]{2,1,0:T(1,128)}), s32[4,1,1024]{2,1,0:T(1,128)S(1)}, u32[]{:S(2)}, u32[]{:S(2)}) async-start(s32[4,1,1024]{2,1,0:T(1,128)} %bitcast.2), calls=%async_computation | async-start | bytes 32768 | tf_op jit(solution)/shard_map/all_to_all | solution.py:83
  49.8 149.5 %all-reduce.2.cloned.1.call-start = ((), (), s32[]{:S(2)}) async-start(), calls=%async_computation.2 | async-start | bytes 131072 | tf_op jit(solution)/shard_map/psum | solution.py:86
  57.0 7.6 %copy-start.3 = (f32[4,128]{1,0:T(4,128)S(1)}, f32[4,128]{1,0:T(4,128)}, u32[]{:S(2)}) copy-start(f32[4,128]{1,0:T(4,128)} %param.13) | copy-start | bytes 6148
  59.9 7.8 %collective-permute-start.4 = (bf16[512,128]{1,0:T(8,128)(2,1)S(1)}, bf16[512,128]{1,0:T(8,128)(2,1)S(1)}, u32[]{:S(2)}, u32[]{:S(2)}) collective-permute-start(bf16[512,128]{1,0:T(8,128)(2,1)S(1)} %broadcast_select_fusion.3), channel_id=1, source_target_pairs={{0,4},{4,8},{8,12},{12,16},{16,20},{20,24},{24,28},{28,0},{1,5},{5... | collective-permute-start | bytes 393224 | tf_op jit(solution)/shard_map/ppermute | solution.py:11
  60.2 7.6 %collective-permute-start.5 = (bf16[512,128]{1,0:T(8,128)(2,1)S(1)}, bf16[512,128]{1,0:T(8,128)(2,1)S(1)}, u32[]{:S(2)}, u32[]{:S(2)}) collective-permute-start(bf16[512,128]{1,0:T(8,128)(2,1)S(1)} %broadcast_select_fusion), channel_id=1, source_target_pairs={{0,28},{4,0},{8,4},{12,8},{16,12},{20,16},{24,20},{28,24},{1,29},{... | collective-permute-start | bytes 393224 | tf_op jit(solution)/shard_map/ppermute | solution.py:11
  84.9 139.0 %all-to-all-start.1 = ((f32[4,1024,128]{2,1,0:T(8,128)}), f32[4,1024,128]{2,1,0:T(8,128)S(1)}, u32[]{:S(2)}, u32[]{:S(2)}) async-start(f32[4,1024,128]{2,1,0:T(8,128)} %bitcast.100), calls=%async_computation.1 | async-start | bytes 4194304 | tf_op jit(solution)/shard_map/all_to_all | solution.py:82
Sparse Core Ops, SparseCore 0:
  78.0 121.1 all-reduce.1
where the time goes:
time: 246 us; the launch traced here: 245 us
  waiting for transfers between devices  116 us (47%)
  local copies, waits for them, and re-layouts  46.9 us (19%)
  other arithmetic  28.5 us (12%)
  starting transfers between devices  23.2 us (9%)
  matrix products  17.4 us (7%)
  between operations  13.7 us (6%)
    psum x1, waiting for transfers between devices, body(): gram = lax.psum(local_gram, ('grp', 'lane'))  109 us
    ppermute x6, starting transfers between devices, from_behind(): lax.ppermute(value, axis, [(i, (i + by) % devices) for i in range(devices)])  13.9 us
    dot_general x3, matrix products, operate(): jnp.einsum('bkij,bkjf->bif', tiles, blocks, preferred_element_type=jnp.fl...  12.8 us
    another operation x3, other arithmetic, body(): factor = jnp.linalg.cholesky(gram)  12.4 us
    scatter x1, local copies, waits for them, and re-layouts, place_rows(): return empty.at[flat_slots].set(received, mode='drop')  11.6 us
    another operation x2, other arithmetic, whiten(): solved = jax.scipy.linalg.solve_triangular(factor, values.T, lower=True).T  10.5 us
    scatter x1, local copies, waits for them, and re-layouts, pack_rows(): jnp.full((lanes * capacity,), row_count, jnp.int32).at[position]  8.78 us
    gather x3, local copies, waits for them, and re-layouts, operate(): blocks = extended[tile_cols]  8.6 us
  transfers between devices with their start and end apart: 9, of which 3 were waited for; matrix products, arithmetic and copies ran while one was open for 26% of the time, Pallas kernels for 0%

commit v1 on v0

--- a/solution.py
+++ b/solution.py
@@ -83,7 +83,7 @@
         lax.all_to_all(raw_slots, "lane", split_axis=0, concat_axis=0, tiled=True),
     )
     local_gram = jnp.einsum("rf,rg->fg", mixed, mixed, precision=lax.Precision.HIGHEST)
-    gram = lax.psum(local_gram, ("grp", "lane"))
+    gram = jnp.sum(lax.all_gather(local_gram, ("grp", "lane")), axis=0)
     factor = jnp.linalg.cholesky(gram)
     flat_raw = received_raw.reshape(-1, feature_width)
     ball_rows = to_ball(whiten(flat_raw, factor, node_total), feature_width)

time: 246 us -> 177 us (0.72)
  waiting for transfers between devices: 116 us -> 45.8 us
    psum x1 -> x0, waiting for transfers between devices: 109 us -> none  [body(): gram = lax.psum(local_gram, ('grp', 'lane'))]
    all_gather x0 -> x1, waiting for transfers between devices: none -> 35.8 us  [body(): gram = jnp.sum(lax.all_gather(local_gram, ('grp', 'lane')), axis=0)]
    ppermute x6, waiting for transfers between devices: 6.42 us -> 9.9 us  [from_behind(): lax.ppermute(value, axis, [(i, (i + by) % devices) for i in range(devices)])]
  transfers between devices with their start and end apart: 9 -> 9, of which waited for: 3 -> 5; matrix products, arithmetic and copies ran while one was open for 26% -> 25% of each run, Pallas kernels for 0% -> 0%
where the time goes in v1:
time: 177 us; the launch traced here: 176 us
  local copies, waits for them, and re-layouts  46 us (26%)
  waiting for transfers between devices  45.8 us (26%)
  other arithmetic  29.4 us (17%)
  starting transfers between devices  24.2 us (14%)
  matrix products  17.4 us (10%)
  between operations  13.7 us (8%)
    all_gather x1, waiting for transfers between devices, body(): gram = jnp.sum(lax.all_gather(local_gram, ('grp', 'lane')), axis=0)  35.8 us
    ppermute x6, starting transfers between devices, from_behind(): lax.ppermute(value, axis, [(i, (i + by) % devices) for i in range(devices)])  13.9 us
    dot_general x3, matrix products, operate(): jnp.einsum('bkij,bkjf->bif', tiles, blocks, preferred_element_type=jnp.fl...  12.8 us
    another operation x3, other arithmetic, body(): factor = jnp.linalg.cholesky(gram)  12.4 us
    scatter x1, local copies, waits for them, and re-layouts, place_rows(): return empty.at[flat_slots].set(received, mode='drop')  11.6 us
    another operation x2, other arithmetic, whiten(): solved = jax.scipy.linalg.solve_triangular(factor, values.T, lower=True).T  10.5 us
    ppermute x6, waiting for transfers between devices, from_behind(): lax.ppermute(value, axis, [(i, (i + by) % devices) for i in range(devices)])  9.9 us
    scatter x1, local copies, waits for them, and re-layouts, pack_rows(): jnp.full((lanes * capacity,), row_count, jnp.int32).at[position]  8.78 us
  transfers between devices with their start and end apart: 9, of which 5 were waited for; matrix products, arithmetic and copies ran while one was open for 25% of the time, Pallas kernels for 0%

profile of v1, /device:TPU:1, one launch (start us, length us, event | category | flops | bytes accessed | tf_op | source)
XLA Modules:
  0.0 176.5 jit_solution(3813342866721215389)
XLA Ops:
  8.1 2.2 %gather_fusion = bf16[512,128]{1,0:T(8,128)(2,1)S(1)} fusion(bf16[2048,128]{1,0:T(8,128)(2,1)} %param.8, s32[1024]{0:T(1024)S(1)} %pad_clamp_fusion.2), kind=kCustom, calls=%fused_computation | custom fusion | bytes 264192 | tf_op jit(solution)/shard_map/gather | solution.py:52
  10.4 2.1 %collective-permute-start = (bf16[512,128]{1,0:T(8,128)(2,1)S(1)}, bf16[512,128]{1,0:T(8,128)(2,1)S(1)}, u32[]{:S(2)}, u32[]{:S(2)}) collective-permute-start(bf16[512,128]{1,0:T(8,128)(2,1)S(1)} %broadcast_select_fusion.5), channel_id=1, source_target_pairs={{0,4},{4,8},{8,12},{12,16},{16,20},{20,24},{24,28},{28,0},{1,5},{5... | collective-permute-start | bytes 393224 | tf_op jit(solution)/shard_map/ppermute | solution.py:11
  12.5 1.3 gather_fusion.1
  14.0 3.1 %collective-permute-start.1 = (bf16[512,128]{1,0:T(8,128)(2,1)S(1)}, bf16[512,128]{1,0:T(8,128)(2,1)S(1)}, u32[]{:S(2)}, u32[]{:S(2)}) collective-permute-start(bf16[512,128]{1,0:T(8,128)(2,1)S(1)} %broadcast_select_fusion.2), channel_id=1, source_target_pairs={{0,28},{4,0},{8,4},{12,8},{16,12},{20,16},{24,20},{28,24},{1,29},{... | collective-permute-start | bytes 393224 | tf_op jit(solution)/shard_map/ppermute | solution.py:11
  17.3 1.4 collective-permute-done
  18.7 3.5 %collective-permute-done.1 = bf16[512,128]{1,0:T(8,128)(2,1)S(1)} collective-permute-done((bf16[512,128]{1,0:T(8,128)(2,1)S(1)}, bf16[512,128]{1,0:T(8,128)(2,1)S(1)}, u32[]{:S(2)}, u32[]{:S(2)}) %collective-permute-start.1) | collective-permute-done | bytes 131104 | tf_op jit(solution)/shard_map/ppermute | solution.py:11
  22.3 2.9 %gather_fusion.2 = bf16[112,128,128]{2,1,0:T(8,128)(2,1)} fusion(bf16[24,128,128]{2,1,0:T(8,128)(2,1)S(1)} %bitcast.99, s32[1024]{0:T(1024)S(1)} %pad_clamp_fusion), kind=kCustom, calls=%fused_computation.2 | custom fusion | bytes 7340480 | tf_op jit(solution)/shard_map/gather | solution.py:62
  25.2 4.3 %fusion.2 = bf16[16,128,128]{1,2,0:T(8,128)(2,1)S(1)} fusion(bf16[16,7,128,128]{3,2,1,0:T(8,128)(2,1)} %param.9, bf16[16,7,128,128]{3,2,1,0:T(8,128)(2,1)} %bitcast.95), kind=kOutput, calls=%fused_computation.23 | convolution fusion | flops 470024192 | bytes 7864320 | tf_op jit(solution)/shard_map/bkij,bkjf->bif/dot_general | solution.py:63
  29.4 1.3 gather_fusion.3
  30.8 1.3 gather_fusion.4
  32.5 4.2 %collective-permute-start.3 = (bf16[512,128]{1,0:T(8,128)(2,1)S(1)}, bf16[512,128]{1,0:T(8,128)(2,1)S(1)}, u32[]{:S(2)}, u32[]{:S(2)}) collective-permute-start(bf16[512,128]{1,0:T(8,128)(2,1)S(1)} %broadcast_select_fusion.1), channel_id=1, source_target_pairs={{0,28},{4,0},{8,4},{12,8},{16,12},{20,16},{24,20},{28,24},{1,29},{... | collective-permute-start | bytes 393224 | tf_op jit(solution)/shard_map/ppermute | solution.py:11
  36.7 2.9 %collective-permute-done.2 = bf16[512,128]{1,0:T(8,128)(2,1)S(1)} collective-permute-done((bf16[512,128]{1,0:T(8,128)(2,1)S(1)}, bf16[512,128]{1,0:T(8,128)(2,1)S(1)}, u32[]{:S(2)}, u32[]{:S(2)}) %collective-permute-start.2) | collective-permute-done | bytes 131104 | tf_op jit(solution)/shard_map/ppermute | solution.py:11
  39.6 2.9 %gather_fusion.5 = bf16[112,128,128]{2,1,0:T(8,128)(2,1)} fusion(bf16[24,128,128]{2,1,0:T(8,128)(2,1)S(1)} %bitcast.100, s32[1024]{0:T(1024)S(1)} %pad_clamp_fusion), kind=kCustom, calls=%fused_computation.5 | custom fusion | bytes 7340480 | tf_op jit(solution)/shard_map/gather | solution.py:62
  42.5 4.3 %fusion = f32[16,128,128]{1,2,0:T(8,128)S(1)} fusion(bf16[16,7,128,128]{3,2,1,0:T(8,128)(2,1)} %param.9, bf16[16,7,128,128]{3,2,1,0:T(8,128)(2,1)} %bitcast.97), kind=kOutput, calls=%fused_computation.17 | convolution fusion | flops 470024192 | bytes 8388608 | tf_op jit(solution)/shard_map/bkij,bkjf->bif/dot_general | solution.py:63
  46.9 1.3 gather_fusion.6
  48.3 1.3 gather_fusion.7
  50.4 4.0 %collective-permute-start.5 = (bf16[512,128]{1,0:T(8,128)(2,1)S(1)}, bf16[512,128]{1,0:T(8,128)(2,1)S(1)}, u32[]{:S(2)}, u32[]{:S(2)}) collective-permute-start(bf16[512,128]{1,0:T(8,128)(2,1)S(1)} %broadcast_select_fusion), channel_id=1, source_target_pairs={{0,28},{4,0},{8,4},{12,8},{16,12},{20,16},{24,20},{28,24},{1,29},{... | collective-permute-start | bytes 393224 | tf_op jit(solution)/shard_map/ppermute | solution.py:11
  54.3 2.1 %collective-permute-done.4 = bf16[512,128]{1,0:T(8,128)(2,1)S(1)} collective-permute-done((bf16[512,128]{1,0:T(8,128)(2,1)S(1)}, bf16[512,128]{1,0:T(8,128)(2,1)S(1)}, u32[]{:S(2)}, u32[]{:S(2)}) %collective-permute-start.4) | collective-permute-done | bytes 131104 | tf_op jit(solution)/shard_map/ppermute | solution.py:11
  56.5 2.9 %gather_fusion.8 = bf16[112,128,128]{2,1,0:T(8,128)(2,1)} fusion(bf16[24,128,128]{2,1,0:T(8,128)(2,1)S(1)} %bitcast.98, s32[1024]{0:T(1024)S(1)} %pad_clamp_fusion), kind=kCustom, calls=%fused_computation.8 | custom fusion | bytes 7340480 | tf_op jit(solution)/shard_map/gather | solution.py:62
  59.3 4.3 %fusion.1 = f32[16,128,128]{1,2,0:T(8,128)S(1)} fusion(bf16[16,7,128,128]{3,2,1,0:T(8,128)(2,1)} %param.9, bf16[16,7,128,128]{3,2,1,0:T(8,128)(2,1)} %bitcast.96), kind=kOutput, calls=%fused_computation.18 | convolution fusion | flops 470024192 | bytes 8388608 | tf_op jit(solution)/shard_map/bkij,bkjf->bif/dot_general | solution.py:63
  64.1 2.5 %fusion.21 = f32[128,128]{1,0:T(8,128)} fusion(f32[2048,128]{1,0:T(8,128)S(1)} %fusion.5), kind=kOutput, calls=%fused_computation.79 | convolution fusion | flops 402653184 | bytes 1114112 | tf_op jit(solution)/shard_map/rf,rg->fg/dot_general | solution.py:85
  66.6 1.2 reduce-window.6
  68.3 8.8 %scatter_custom_fusion = s32[4096]{0:T(1024)} fusion(s32[2048]{0:T(1024)S(1)} %compare_select_fusion.1, s32[2048]{0:T(1024)} %param.15, s32[]{:T(128)} %constant.66.clone.1), kind=kCustom, calls=%fused_computation.66 | custom fusion | bytes 16896 | tf_op jit(solution)/shard_map/scatter | solution.py:31
  77.1 6.5 %all-to-all-start = ((s32[4,1,1024]{2,1,0:T(1,128)}), s32[4,1,1024]{2,1,0:T(1,128)S(1)}, u32[]{:S(2)}, u32[]{:S(2)}) async-start(s32[4,1,1024]{2,1,0:T(1,128)} %bitcast.2), calls=%async_computation | async-start | bytes 32768 | tf_op jit(solution)/shard_map/all_to_all | solution.py:83
  83.6 7.0 %scatter_custom_fusion.1 = f32[4096,128]{1,0:T(8,128)} fusion(s32[2048]{0:T(1024)S(1)} %compare_select_fusion.1, f32[2048,128]{1,0:T(8,128)S(1)} %fusion.5, f32[]{:T(128)} %constant.71.clone.1), kind=kCustom, calls=%fused_computation.29 | custom fusion | bytes 2097156 | tf_op jit(solution)/shard_map/scatter | solution.py:30
  90.5 3.8 %all-to-all-start.1 = ((f32[4,1024,128]{2,1,0:T(8,128)}), f32[4,1024,128]{2,1,0:T(8,128)S(1)}, u32[]{:S(2)}, u32[]{:S(2)}) async-start(f32[4,1024,128]{2,1,0:T(8,128)} %bitcast.101), calls=%async_computation.1 | async-start | bytes 4194304 | tf_op jit(solution)/shard_map/all_to_all | solution.py:82
  94.4 35.8 %all-gather.3.cloned.1.call-done = f32[4096,128]{1,0:T(8,128)} async-done(((f32[128,128]{1,0:T(8,128)}), f32[4096,128]{1,0:T(8,128)}) %all-gather.3.cloned.1.call-update) | async-done | bytes 2097168 | tf_op jit(solution)/shard_map/all_gather | solution.py:86
  130.2 1.7 reduce_sum.28
  132.0 11.7 %cholesky.16 = f32[128,128]{1,0:T(8,128)S(1)} custom-call(f32[128,128]{1,0:T(8,128)S(1)} %fusion.15), custom_call_target="Cholesky" | custom-call | tf_op jit(solution)/shard_map/jit(cholesky)/cholesky | solution.py:87
  145.1 9.8 %custom-call.7 = f32[1,128,128]{1,2,0:T(8,128)S(1)} custom-call(f32[1,128,128]{2,1,0:T(8,128)S(1)} %fusion.12), custom_call_target="InvertDiagBlocksLowerTriangular" | custom-call | tf_op jit(solution)/shard_map/jit(_solve_triangular)/triangular_solve | solution.py:21
  154.9 2.2 %multiply_reduce_fusion = (f32[4096]{0:T(1024)S(1)}, f32[4096,128]{0,1:T(8,128)S(1)}) fusion(f32[4096,128]{1,0:T(8,128)S(1)} %bitcast.102, f32[1,128,128]{1,2,0:T(8,128)S(1)} %custom-call.7), kind=kOutput, calls=%fused_computation.13 | convolution fusion | flops 806875136 | bytes 4276224 | tf_op jit(solution)/shard_map/jit(_solve_triangular)/triangular_solve | solution.py:21
  158.0 11.6 %scatter_custom_fusion.2 = bf16[2048,128]{1,0:T(8,128)(2,1)} fusion(s32[4096]{0:T(1024)S(1)} %bitcast.106, bf16[4096,128]{1,0:T(8,128)(2,1)S(1)} %copy.16, bf16[]{:T(256)} %constant.65.clone.1), kind=kCustom, calls=%fused_computation.34 | custom fusion | bytes 524290 | tf_op jit(solution)/shard_map/scatter | solution.py:38
  (52 shorter events, 6.8 us)
Async XLA Ops:
  6.5 6.0 %copy-start = (bf16[2048,128]{1,0:T(8,128)(2,1)S(1)}, bf16[2048,128]{1,0:T(8,128)(2,1)}, u32[]{:S(2)}) copy-start(bf16[2048,128]{1,0:T(8,128)(2,1)} %param.8) | copy-start | bytes 1572868
  6.5 10.6 %copy-start.2 = (s32[16,7]{0,1:T(8,128)S(1)}, s32[16,7]{0,1:T(8,128)}, u32[]{:S(2)}) copy-start(s32[16,7]{0,1:T(8,128)} %param.10) | copy-start | bytes 1348
  6.5 123.7 %all-gather.3.cloned.1.call-start = ((), (), s32[]{:S(2)}) async-start(), calls=%async_computation.2 | async-start | bytes 2162688 | tf_op jit(solution)/shard_map/all_gather | solution.py:86
  10.4 8.4 %collective-permute-start = (bf16[512,128]{1,0:T(8,128)(2,1)S(1)}, bf16[512,128]{1,0:T(8,128)(2,1)S(1)}, u32[]{:S(2)}, u32[]{:S(2)}) collective-permute-start(bf16[512,128]{1,0:T(8,128)(2,1)S(1)} %broadcast_select_fusion.5), channel_id=1, source_target_pairs={{0,4},{4,8},{8,12},{12,16},{16,20},{20,24},{24,28},{28,0},{1,5},{5... | collective-permute-start | bytes 393224 | tf_op jit(solution)/shard_map/ppermute | solution.py:11
  14.0 8.3 %collective-permute-start.1 = (bf16[512,128]{1,0:T(8,128)(2,1)S(1)}, bf16[512,128]{1,0:T(8,128)(2,1)S(1)}, u32[]{:S(2)}, u32[]{:S(2)}) collective-permute-start(bf16[512,128]{1,0:T(8,128)(2,1)S(1)} %broadcast_select_fusion.2), channel_id=1, source_target_pairs={{0,28},{4,0},{8,4},{12,8},{16,12},{20,16},{24,20},{28,24},{1,29},{... | collective-permute-start | bytes 393224 | tf_op jit(solution)/shard_map/ppermute | solution.py:11
  32.3 7.3 %collective-permute-start.2 = (bf16[512,128]{1,0:T(8,128)(2,1)S(1)}, bf16[512,128]{1,0:T(8,128)(2,1)S(1)}, u32[]{:S(2)}, u32[]{:S(2)}) collective-permute-start(bf16[512,128]{1,0:T(8,128)(2,1)S(1)} %broadcast_select_fusion.4), channel_id=1, source_target_pairs={{0,4},{4,8},{8,12},{12,16},{16,20},{20,24},{24,28},{28,0},{1,5},{5... | collective-permute-start | bytes 393224 | tf_op jit(solution)/shard_map/ppermute | solution.py:11
  32.5 7.1 %collective-permute-start.3 = (bf16[512,128]{1,0:T(8,128)(2,1)S(1)}, bf16[512,128]{1,0:T(8,128)(2,1)S(1)}, u32[]{:S(2)}, u32[]{:S(2)}) collective-permute-start(bf16[512,128]{1,0:T(8,128)(2,1)S(1)} %broadcast_select_fusion.1), channel_id=1, source_target_pairs={{0,28},{4,0},{8,4},{12,8},{16,12},{20,16},{24,20},{28,24},{1,29},{... | collective-permute-start | bytes 393224 | tf_op jit(solution)/shard_map/ppermute | solution.py:11
  46.8 7.6 %copy-start.3 = (f32[4,128]{1,0:T(4,128)S(1)}, f32[4,128]{1,0:T(4,128)}, u32[]{:S(2)}) copy-start(f32[4,128]{1,0:T(4,128)} %param.13) | copy-start | bytes 6148
  49.7 6.7 %collective-permute-start.4 = (bf16[512,128]{1,0:T(8,128)(2,1)S(1)}, bf16[512,128]{1,0:T(8,128)(2,1)S(1)}, u32[]{:S(2)}, u32[]{:S(2)}) collective-permute-start(bf16[512,128]{1,0:T(8,128)(2,1)S(1)} %broadcast_select_fusion.3), channel_id=1, source_target_pairs={{0,4},{4,8},{8,12},{12,16},{16,20},{20,24},{24,28},{28,0},{1,5},{5... | collective-permute-start | bytes 393224 | tf_op jit(solution)/shard_map/ppermute | solution.py:11
  50.4 6.1 %collective-permute-start.5 = (bf16[512,128]{1,0:T(8,128)(2,1)S(1)}, bf16[512,128]{1,0:T(8,128)(2,1)S(1)}, u32[]{:S(2)}, u32[]{:S(2)}) collective-permute-start(bf16[512,128]{1,0:T(8,128)(2,1)S(1)} %broadcast_select_fusion), channel_id=1, source_target_pairs={{0,28},{4,0},{8,4},{12,8},{16,12},{20,16},{24,20},{28,24},{1,29},{... | collective-permute-start | bytes 393224 | tf_op jit(solution)/shard_map/ppermute | solution.py:11
  63.6 2.9 %copy-start.1 = (s32[2048]{0:T(1024)S(1)}, s32[2048]{0:T(1024)}, u32[]{:S(2)}) copy-start(s32[2048]{0:T(1024)} %param.14) | copy-start | bytes 24580
  77.1 13.5 %all-to-all-start = ((s32[4,1,1024]{2,1,0:T(1,128)}), s32[4,1,1024]{2,1,0:T(1,128)S(1)}, u32[]{:S(2)}, u32[]{:S(2)}) async-start(s32[4,1,1024]{2,1,0:T(1,128)} %bitcast.2), calls=%async_computation | async-start | bytes 32768 | tf_op jit(solution)/shard_map/all_to_all | solution.py:83
  90.5 64.4 %all-to-all-start.1 = ((f32[4,1024,128]{2,1,0:T(8,128)}), f32[4,1024,128]{2,1,0:T(8,128)S(1)}, u32[]{:S(2)}, u32[]{:S(2)}) async-start(f32[4,1024,128]{2,1,0:T(8,128)} %bitcast.101), calls=%async_computation.1 | async-start | bytes 4194304 | tf_op jit(solution)/shard_map/all_to_all | solution.py:82
Sparse Core Ops, SparseCore 0:
  66.7 63.4 all-gather.2
